TPU v7x, 128 devices: a whole 4x4x4 slice. The times are simulated.
128 devices in a mesh: fsdp: 8 (over y_lo, z), ctx: 4 (over y_hi, core), tp: 4 (over x).
Axes of the slice: x: 4, y: 4 (y_hi: 2, y_lo: 2; y = y_hi * 2 + y_lo), z: 4, core: 2. Of those that a mesh axis runs over, the one named last changes fastest.
Arguments:
- inputs: bfloat16 [32, 1024, 960], P(('fsdp', 'tp'), 'ctx'), may hold values from -6 to 6
- seq_live: int32 [32], P(('fsdp', 'tp')), may hold values from 0 to 1, as said below
- positions: int32 [32, 1024], P(('fsdp', 'tp'), 'ctx'), may hold values from 0 to 2046, as said below
- gain_attn: bfloat16 [960], P('fsdp'), may hold values from 0.5 to 1.5
- w_query: bfloat16 [960, 960], P('fsdp'), may hold values from -0.75 to 0.75
- w_key: bfloat16 [960, 320], P('fsdp'), may hold values from -0.75 to 0.75
- w_value: bfloat16 [960, 320], P('fsdp'), may hold values from -0.1875 to 0.1875
- w_out: bfloat16 [960, 960], P('fsdp'), may hold values from -1.5 to 1.5
- gain_mlp: bfloat16 [960], P('fsdp'), may hold values from 0.5 to 1.5
- w_gate: bfloat16 [960, 2560], P('fsdp', 'tp'), may hold values from -0.1875 to 0.1875
- w_up: bfloat16 [960, 2560], P('fsdp', 'tp'), may hold values from -0.1875 to 0.1875
- w_down: bfloat16 [960, 2560], P('fsdp', 'tp'), may hold values from -0.125 to 0.125
- cotangent: float32 [32, 1024, 960], P(('fsdp', 'tp'), 'ctx'), may hold values from -6 to 6
Outputs:
- layer_out: float32 [32, 1024, 960], P(('fsdp', 'tp'), 'ctx')
- dinputs: float32 [32, 1024, 960], P(('fsdp', 'tp'), 'ctx')
- dgain_attn: float32 [960], P('fsdp')
- dw_query: float32 [960, 960], P('fsdp')
- dw_key: float32 [960, 320], P('fsdp')
- dw_value: float32 [960, 320], P('fsdp')
- dw_out: float32 [960, 960], P('fsdp')
- dgain_mlp: float32 [960], P('fsdp')
- dw_gate: float32 [960, 2560], P('fsdp', 'tp')
- dw_up: float32 [960, 2560], P('fsdp', 'tp')
- dw_down: float32 [960, 2560], P('fsdp', 'tp')
Inputs may be any that keep to these rules, and one draw needn't show every extreme that they name: `seq_live`: the slots fall into equal blocks of consecutive slots, one block for each index of fsdp; each block holds either only 1s or exactly one 0, at any slot of the block, and both kinds of block occur. `positions`: each row starts at 0 and rises by 1 or 2 from token to token; the first slot's row rises by 2 throughout.
All inputs are finite; a program needn't handle non-finite values.
Results may differ from a plain program's by a relative error of at most 0.025.
Values may be sent and summed in bfloat16 or wider, within the bound.
No kernel may reach another device: no remote copies, remote signals or barrier semaphores. Data moves between devices by JAX's collectives and lax.ppermute only.
A program may use at most 128 MiB of HBM per device.

v0:
```python
import math
import jax
import jax.numpy as jnp
from jax import lax
from jax.sharding import PartitionSpec as P

QH = 15
KVH = 5
HEAD = 64
EPSILON = 1e-05
ROPE_BASE = 100000.0


def joined_along(tiles, dim):
    tiles = jnp.moveaxis(tiles, 0, dim)
    lengths = tiles.shape
    return tiles.reshape(*lengths[:dim], lengths[dim] * lengths[dim + 1], *lengths[dim + 2 :])


def from_everyone(shard, axis):
    copies = jnp.broadcast_to(shard, (lax.axis_size(axis), *shard.shape))
    return lax.all_to_all(copies, axis, split_axis=0, concat_axis=0, tiled=True)


def collect(shard, axis, dim):
    return joined_along(from_everyone(shard, axis), dim)


def cut_along(shard, dim, devices):
    lengths = shard.shape
    tiles = shard.reshape(*lengths[:dim], devices, lengths[dim] // devices, *lengths[dim + 1 :])
    return jnp.moveaxis(tiles, dim, 0)


def sent_and_summed(shard, axis, dim):
    tiles = cut_along(shard, dim, lax.axis_size(axis))
    arrived = lax.all_to_all(tiles, axis, split_axis=0, concat_axis=0, tiled=True)
    return arrived.astype(jnp.float32).sum(axis=0)


def sum_at_owner(shard, axis, dim):
    tiles = cut_along(shard, dim, lax.axis_size(axis))
    arrived = lax.all_to_all(tiles, axis, split_axis=0, concat_axis=0, tiled=True)
    return arrived.sum(axis=0)


def sent_together(arrays, axis, dim, along):
    columns = [a.reshape(*a.shape[:along], -1) for a in arrays]
    both = jnp.concatenate(columns, axis=along)
    out, at, done = (lax.psum_scatter(both, axis, scatter_dimension=dim, tiled=True), 0, [])
    for a, column in zip(arrays, columns):
        slab = out[..., at : at + column.shape[along]]
        done.append(slab.reshape(*slab.shape[:along], *a.shape[along:]))
        at += column.shape[along]
    return tuple(done)


def over_copies(shard, axis):
    return from_everyone(shard, axis).astype(jnp.float32).sum(axis=0)


def rope_tables(position_ids):
    half_dim = HEAD // 2
    freq_index = jnp.arange(half_dim, dtype=jnp.float32)
    inverse = jnp.exp(freq_index * (-2.0 * math.log(ROPE_BASE) / HEAD))
    angles = position_ids.astype(jnp.float32)[:, None] * inverse[None, :]
    return (jnp.cos(angles)[:, None, :], jnp.sin(angles)[:, None, :])


def rotate(tensor, cos_table, sin_table):
    half_dim = tensor.shape[-1] // 2
    first_half = tensor[..., :half_dim]
    second_half = tensor[..., half_dim:]
    return jnp.concatenate(
        [
            first_half * cos_table - second_half * sin_table,
            second_half * cos_table + first_half * sin_table,
        ],
        -1,
    )


def rotate_back(tensor, cos_table, sin_table):
    half_dim = tensor.shape[-1] // 2
    first_half = tensor[..., :half_dim]
    second_half = tensor[..., half_dim:]
    return jnp.concatenate(
        [
            first_half * cos_table + second_half * sin_table,
            second_half * cos_table - first_half * sin_table,
        ],
        -1,
    )


def rms_forward(stream, gain_vector):
    scale_inv = lax.rsqrt(jnp.mean(stream * stream, -1, keepdims=True) + EPSILON)
    normed = stream * scale_inv
    return (scale_inv, normed, (normed * gain_vector.astype(jnp.float32)).astype(jnp.bfloat16))


def rms_backward(upstream, scale_inv, normed, gain_vector):
    scaled = upstream * gain_vector.astype(jnp.float32)
    inner_mean = jnp.mean(scaled * normed, -1, keepdims=True)
    return (scale_inv * (scaled - normed * inner_mean), jnp.sum(upstream * normed, 0))


def masked_scores(head_queries, head_keys, allowed, score_scale):
    scores = (
        jnp.einsum("sqgd,skd->sgqk", head_queries, head_keys, preferred_element_type=jnp.float32)
        * score_scale
    )
    return jnp.where(allowed, scores, -1e30)


def shards(
    inputs,
    seq_live,
    positions,
    gain_attn,
    w_query,
    w_key,
    w_value,
    w_out,
    gain_mlp,
    w_gate,
    w_up,
    w_down,
    cotangent,
):
    (
        full_gain_attn,
        full_gain_mlp,
        full_query,
        full_key,
        full_value,
        full_out,
        full_gate,
        full_up,
        full_down,
    ) = (
        lax.all_gather(gain_attn, "fsdp", axis=0, tiled=True),
        lax.all_gather(gain_mlp, "fsdp", axis=0, tiled=True),
        lax.all_gather(w_query, "fsdp", axis=0, tiled=True),
        lax.all_gather(w_key, "fsdp", axis=0, tiled=True),
        lax.all_gather(w_value, "fsdp", axis=0, tiled=True),
        lax.all_gather(w_out, "fsdp", axis=0, tiled=True),
        lax.all_gather(w_gate, "fsdp", axis=0, tiled=True),
        lax.all_gather(w_up, "fsdp", axis=0, tiled=True),
        lax.all_gather(w_down, "fsdp", axis=0, tiled=True),
    )
    seq_dev, local_len, model_width = inputs.shape
    full_len = local_len * lax.axis_size("ctx")
    row_count = seq_dev * local_len
    group_size = QH // KVH
    kv_dim = KVH * HEAD
    score_scale = 1.0 / math.sqrt(HEAD)
    contract_rows = (((0,), (0,)), ((), ()))
    contract_cols = (((1,), (1,)), ((), ()))
    stream = inputs.astype(jnp.float32).reshape(row_count, model_width)
    inv_one, normed_one, hidden_one = rms_forward(stream, full_gain_attn)
    cos_table, sin_table = rope_tables(positions.reshape(row_count))
    query_lin = jnp.dot(hidden_one, full_query, preferred_element_type=jnp.float32).reshape(
        row_count, QH, HEAD
    )
    queries = rotate(query_lin, cos_table, sin_table).astype(jnp.bfloat16)
    key_lin = jnp.dot(hidden_one, full_key, preferred_element_type=jnp.float32).reshape(
        row_count, KVH, HEAD
    )
    key_rows = rotate(key_lin, cos_table, sin_table).astype(jnp.bfloat16)
    value_rows = jnp.dot(hidden_one, full_value, preferred_element_type=jnp.float32).astype(
        jnp.bfloat16
    )
    packed = jnp.concatenate([key_rows.reshape(row_count, kv_dim), value_rows], 1).reshape(
        seq_dev, local_len, 2 * kv_dim
    )
    gathered = collect(packed, "ctx", 1)
    all_keys = gathered[..., :kv_dim].reshape(seq_dev, full_len, KVH, HEAD)
    all_values = gathered[..., kv_dim:].reshape(seq_dev, full_len, KVH, HEAD)
    query_groups = queries.reshape(seq_dev, local_len, KVH, group_size, HEAD)
    query_index = lax.axis_index("ctx") * local_len + jnp.arange(local_len, dtype=jnp.int32)
    allowed = query_index[:, None] >= jnp.arange(full_len, dtype=jnp.int32)[None, :]
    log_totals = []
    attended_parts = []
    for head_index in range(KVH):
        scores = masked_scores(
            query_groups[:, :, head_index], all_keys[:, :, head_index], allowed, score_scale
        )
        row_top = jnp.max(scores, -1, keepdims=True)
        log_total = row_top + jnp.log(jnp.sum(jnp.exp(scores - row_top), -1, keepdims=True))
        probs_b = jnp.exp(scores - log_total).astype(jnp.bfloat16)
        attended_parts.append(
            jnp.einsum(
                "sgqk,skd->sqgd",
                probs_b,
                all_values[:, :, head_index],
                preferred_element_type=jnp.float32,
            )
        )
        log_totals.append(log_total)
    attended = jnp.stack(attended_parts, 2).astype(jnp.bfloat16).reshape(row_count, QH * HEAD)
    mid_stream = stream + jnp.dot(attended, full_out, preferred_element_type=jnp.float32)
    inv_two, normed_two, hidden_two = rms_forward(mid_stream, full_gain_mlp)
    mlp_input = collect(hidden_two.reshape(seq_dev, local_len, model_width), "tp", 0).reshape(
        -1, model_width
    )
    gate_pre = jnp.dot(mlp_input, full_gate, preferred_element_type=jnp.float32)
    up_pre = jnp.dot(mlp_input, full_up, preferred_element_type=jnp.float32)
    sigmoid_gate = jax.nn.sigmoid(gate_pre)
    activated = (gate_pre * sigmoid_gate * up_pre).astype(jnp.bfloat16)
    partial_out = lax.dot_general(
        activated, full_down, contract_cols, preferred_element_type=jnp.float32
    )
    mlp_out = sent_and_summed(
        partial_out.reshape(-1, local_len, model_width).astype(jnp.bfloat16), "tp", 0
    ).reshape(row_count, model_width)
    layer_out = mid_stream + mlp_out
    upstream = (cotangent * seq_live.astype(jnp.float32)[:, None, None]).reshape(
        row_count, model_width
    )
    upstream_b = upstream.astype(jnp.bfloat16)
    grad_rows = collect(upstream_b.reshape(seq_dev, local_len, model_width), "tp", 0).reshape(
        -1, model_width
    )
    grad_act = jnp.dot(grad_rows, full_down, preferred_element_type=jnp.float32)
    up_back = (grad_act * gate_pre * sigmoid_gate).astype(jnp.bfloat16)
    gate_back = (grad_act * up_pre * sigmoid_gate * (1.0 + gate_pre * (1.0 - sigmoid_gate))).astype(
        jnp.bfloat16
    )
    grad_down_full = lax.dot_general(
        grad_rows, activated, contract_rows, preferred_element_type=jnp.float32
    )
    grad_gate_full = lax.dot_general(
        mlp_input, gate_back, contract_rows, preferred_element_type=jnp.float32
    )
    grad_up_full = lax.dot_general(
        mlp_input, up_back, contract_rows, preferred_element_type=jnp.float32
    )
    partial_in = lax.dot_general(
        gate_back, full_gate, contract_cols, preferred_element_type=jnp.float32
    ) + lax.dot_general(up_back, full_up, contract_cols, preferred_element_type=jnp.float32)
    grad_hidden_two = sum_at_owner(partial_in.reshape(-1, local_len, model_width), "tp", 0).reshape(
        row_count, model_width
    )
    back_two, grad_gain_two = rms_backward(grad_hidden_two, inv_two, normed_two, full_gain_mlp)
    grad_mid = upstream + back_two
    grad_mid_b = grad_mid.astype(jnp.bfloat16)
    grad_out_full = lax.dot_general(
        attended, grad_mid_b, contract_rows, preferred_element_type=jnp.float32
    )
    grad_attended = lax.dot_general(
        grad_mid_b, full_out, contract_cols, preferred_element_type=jnp.float32
    ).astype(jnp.bfloat16)
    grad_attended = grad_attended.reshape(seq_dev, local_len, KVH, group_size, HEAD)
    key_grad_parts = []
    value_grad_parts = []
    query_grad_parts = []
    for head_index in range(KVH):
        head_queries = query_groups[:, :, head_index]
        head_keys = all_keys[:, :, head_index]
        head_values = all_values[:, :, head_index]
        head_grads = grad_attended[:, :, head_index]
        scores = masked_scores(head_queries, head_keys, allowed, score_scale)
        softmax = jnp.exp(scores - log_totals[head_index])
        probs_b = softmax.astype(jnp.bfloat16)
        grad_probs = jnp.einsum(
            "sqgd,skd->sgqk", head_grads, head_values, preferred_element_type=jnp.float32
        )
        row_inner = jnp.sum(softmax * grad_probs, -1, keepdims=True)
        grad_scores = (softmax * (grad_probs - row_inner) * score_scale).astype(jnp.bfloat16)
        value_grad_parts.append(
            jnp.einsum("sgqk,sqgd->skd", probs_b, head_grads, preferred_element_type=jnp.float32)
        )
        key_grad_parts.append(
            jnp.einsum(
                "sgqk,sqgd->skd", grad_scores, head_queries, preferred_element_type=jnp.float32
            )
        )
        query_grad_parts.append(
            jnp.einsum("sgqk,skd->sqgd", grad_scores, head_keys, preferred_element_type=jnp.float32)
        )
    grad_keys_all = jnp.stack(key_grad_parts, 2).reshape(seq_dev, full_len, kv_dim)
    grad_values_all = jnp.stack(value_grad_parts, 2).reshape(seq_dev, full_len, kv_dim)
    grad_queries = jnp.stack(query_grad_parts, 2).reshape(row_count, QH, HEAD)
    packed_grads = jnp.concatenate([grad_keys_all, grad_values_all], -1)
    own_grads = sum_at_owner(packed_grads, "ctx", 1).reshape(row_count, 2 * kv_dim)
    grad_key_lin = (
        rotate_back(own_grads[:, :kv_dim].reshape(row_count, KVH, HEAD), cos_table, sin_table)
        .astype(jnp.bfloat16)
        .reshape(row_count, kv_dim)
    )
    grad_value_lin = own_grads[:, kv_dim:].astype(jnp.bfloat16)
    grad_query_lin = (
        rotate_back(grad_queries, cos_table, sin_table)
        .astype(jnp.bfloat16)
        .reshape(row_count, QH * HEAD)
    )
    grad_query_full = lax.dot_general(
        hidden_one, grad_query_lin, contract_rows, preferred_element_type=jnp.float32
    )
    grad_key_full = lax.dot_general(
        hidden_one, grad_key_lin, contract_rows, preferred_element_type=jnp.float32
    )
    grad_value_full = lax.dot_general(
        hidden_one, grad_value_lin, contract_rows, preferred_element_type=jnp.float32
    )
    grad_hidden_one = lax.dot_general(
        grad_query_lin, full_query, contract_cols, preferred_element_type=jnp.float32
    )
    grad_hidden_one = grad_hidden_one + lax.dot_general(
        grad_key_lin, full_key, contract_cols, preferred_element_type=jnp.float32
    )
    grad_hidden_one = grad_hidden_one + lax.dot_general(
        grad_value_lin, full_value, contract_cols, preferred_element_type=jnp.float32
    )
    back_one, grad_gain_one = rms_backward(grad_hidden_one, inv_one, normed_one, full_gain_attn)
    grad_input = grad_mid + back_one
    (
        share_gain_one,
        share_gain_two,
        share_query,
        share_key,
        share_value,
        share_out,
        share_gate,
        share_up,
        share_down,
    ) = (
        lax.psum_scatter(
            grad_gain_one.astype(jnp.bfloat16), "fsdp", scatter_dimension=0, tiled=True
        ).astype(jnp.float32),
        *tuple(
            (
                part.astype(jnp.float32)
                for part in sent_together(
                    (
                        grad_gain_two.astype(jnp.bfloat16),
                        grad_query_full.astype(jnp.bfloat16),
                        grad_key_full.astype(jnp.bfloat16),
                        grad_value_full.astype(jnp.bfloat16),
                        grad_out_full.astype(jnp.bfloat16),
                        grad_gate_full.astype(jnp.bfloat16),
                        grad_up_full.astype(jnp.bfloat16),
                        grad_down_full.astype(jnp.bfloat16),
                    ),
                    "fsdp",
                    0,
                    1,
                )
            )
        ),
    )
    share_gate, share_up, share_down = (
        over_copies(share_gate.astype(jnp.bfloat16), "ctx").astype(jnp.float32),
        over_copies(share_up.astype(jnp.bfloat16), "ctx").astype(jnp.float32),
        over_copies(share_down.astype(jnp.bfloat16), "ctx").astype(jnp.float32),
    )
    share_gain_one, share_gain_two, share_query, share_key, share_value, share_out = (
        lax.psum(share_gain_one.astype(jnp.bfloat16), ("ctx", "tp")).astype(jnp.float32),
        lax.psum(share_gain_two.astype(jnp.bfloat16), ("ctx", "tp")).astype(jnp.float32),
        lax.psum(share_query.astype(jnp.bfloat16), ("ctx", "tp")).astype(jnp.float32),
        lax.psum(share_key.astype(jnp.bfloat16), ("ctx", "tp")).astype(jnp.float32),
        lax.psum(share_value.astype(jnp.bfloat16), ("ctx", "tp")).astype(jnp.float32),
        lax.psum(share_out.astype(jnp.bfloat16), ("ctx", "tp")).astype(jnp.float32),
    )
    return (
        layer_out.reshape(seq_dev, local_len, model_width),
        grad_input.reshape(seq_dev, local_len, model_width),
        share_gain_one,
        share_query,
        share_key,
        share_value,
        share_out,
        share_gain_two,
        share_gate,
        share_up,
        share_down,
    )


def solution(mesh):
    placed = (
        P(("fsdp", "tp"), "ctx", None),
        P(("fsdp", "tp")),
        P(("fsdp", "tp"), "ctx"),
        P("fsdp"),
        P("fsdp", None),
        P("fsdp", None),
        P("fsdp", None),
        P("fsdp", None),
        P("fsdp"),
        P("fsdp", "tp"),
        P("fsdp", "tp"),
        P("fsdp", "tp"),
        P(("fsdp", "tp"), "ctx", None),
    )
    return jax.shard_map(
        shards,
        mesh=mesh,
        in_specs=placed,
        out_specs=(
            P(("fsdp", "tp"), "ctx", None),
            P(("fsdp", "tp"), "ctx", None),
            P("fsdp"),
            P("fsdp", None),
            P("fsdp", None),
            P("fsdp", None),
            P("fsdp", None),
            P("fsdp"),
            P("fsdp", "tp"),
            P("fsdp", "tp"),
            P("fsdp", "tp"),
        ),
        check_vma=False,
    )
```

profile of v0, /device:TPU:0, one launch (start us, length us, event | category | flops | bytes accessed | tf_op | source)
XLA Modules:
  0.0 709.2 jit_solution(10042288850751372710)
XLA Ops:
  9.4 31.9 %all-gather = bf16[8,120,320]{1,2,0:T(8,128)(2,1)S(1)} all-gather(bf16[1,120,320]{1,2,0:T(8,128)(2,1)} %bitcast.612), channel_id=1, replica_groups=mesh['fsdp'=8,'ctx'=4,'tp'=4] {'fsdp'}, dimensions={0}, use_global_device_ids=true | all-gather | bytes 691200 | tf_op jit(solution)/shard_map/all_gather | solution.py:145
  41.3 31.0 %all-gather.1 = bf16[8,120,320]{1,2,0:T(8,128)(2,1)S(1)} all-gather(bf16[1,120,320]{1,2,0:T(8,128)(2,1)} %bitcast.613), channel_id=1, replica_groups=mesh['fsdp'=8,'ctx'=4,'tp'=4] {'fsdp'}, dimensions={0}, use_global_device_ids=true | all-gather | bytes 691200 | tf_op jit(solution)/shard_map/all_gather | solution.py:146
  76.7 18.3 %all-reduce.5 = (bf16[960]{0:T(1024)(128)(2,1)S(1)}, bf16[960]{0:T(1024)(128)(2,1)S(1)}) all-reduce(bf16[960]{0:T(1024)(128)(2,1)S(1)} %dynamic-update-slice, bf16[960]{0:T(1024)(128)(2,1)S(1)} %dynamic-update-slice.1), channel_id=1, replica_groups=mesh['fsdp'=8,'ctx'=4,'tp'=4] {'fsdp'}, use_global_device_ids=true, to_apply=%add | all-reduce | flops 1920 | bytes 7680
  99.5 4.7 all-to-all-start
  106.5 25.6 %all-to-all-done = bf16[4,1,256,640]{2,3,1,0:T(8,128)(2,1)S(1)} async-done(((bf16[4,1,256,640]{2,3,1,0:T(8,128)(2,1)}), bf16[4,1,256,640]{2,3,1,0:T(8,128)(2,1)S(1)}, u32[]{:S(2)}, u32[]{:S(2)}) %all-to-all-start) | async-done | bytes 1310752 | tf_op jit(solution)/shard_map/all_to_all | solution.py:22
  132.1 2.4 broadcast_in_dim.78
  134.6 5.3 all-to-all-start.3
  141.8 2.3 copy.190
  144.4 3.1 copy.192
  149.2 2.2 fusion.128
  162.9 2.7 multiply_reduce_fusion.2
  167.6 2.4 broadcast_in_dim.77
  170.0 4.8 all-to-all-start.1
  175.4 3.1 copy.200
  180.2 18.0 %all-to-all-done.1 = bf16[4,1,256,960]{2,3,1,0:T(8,128)(2,1)} async-done(((bf16[4,1,256,960]{2,3,1,0:T(8,128)(2,1)}), bf16[4,1,256,960]{2,3,1,0:T(8,128)(2,1)}, u32[]{:S(2)}, u32[]{:S(2)}) %all-to-all-start.1) | async-done | bytes 1966112 | tf_op jit(solution)/shard_map/all_to_all | solution.py:22
  198.2 3.1 copy.198
  203.0 5.3 fusion.133
  208.3 5.2 fusion.132
  213.5 6.0 all-gather.16.cloned.1.call-done
  219.6 7.8 %multiply_convert_fusion = (bf16[1024,640]{1,0:T(8,128)(2,1)}, bf16[1024,640]{1,0:T(8,128)(2,1)}, bf16[1024,640]{1,0:T(8,128)(2,1)S(1)}) fusion(f32[1024,640]{1,0:T(8,128)} %fusion.132, f32[1024,640]{1,0:T(8,128)} %fusion.133, bf16[1024,960]{0,1:T(8,128)(2,1)} %bitcast.598, bf16[960,640]{1,0:T(8,128)(2,1)} %all-gather.16.cloned.1.call-done), kind=kOutput, calls=%fused_computation.47 | convolution fusion | flops 1268776960 | bytes 12369920 | tf_op jit(solution)/shard_map/dot_general | solution.py:225
  228.4 3.0 convolution_convert_fusion.2
  231.5 4.7 convert_element_type.260
  236.1 3.1 copy.199
  239.2 4.5 all-to-all-start.2
  243.7 3.5 fusion.134
  247.3 3.6 convolution_add_fusion
  250.9 5.4 reshape_reshape.11
  256.3 4.7 copy.201
  261.1 2.9 all-to-all-done.2
  264.0 5.0 all-to-all-start.4
  269.0 4.8 convolution_convert_fusion.3
  273.8 2.7 convolution_convert_fusion.4
  276.5 2.8 convolution_convert_fusion.5
  279.3 2.9 convert_reduce_fusion
  282.2 26.7 %all-to-all-done.4 = f32[4,1,256,960]{2,3,1,0:T(8,128)} async-done(((f32[4,1,256,960]{2,3,1,0:T(8,128)}), f32[4,1,256,960]{2,3,1,0:T(8,128)}, u32[]{:S(2)}, u32[]{:S(2)}) %all-to-all-start.4) | async-done | bytes 3932192 | tf_op jit(solution)/shard_map/all_to_all | solution.py:43
  308.9 3.4 reduce_sum.206
  312.3 2.0 multiply_reduce_fusion
  314.4 2.9 bitcast_add_fusion
  320.9 2.3 fusion
  323.5 2.2 fusion.4
  326.2 2.3 fusion.8
  328.5 2.2 fusion.12
  341.8 2.8 concatenate.49
  344.6 2.7 copy.218
  347.3 3.7 fusion.34
  368.0 4.7 all-to-all-start.5
  372.8 2.7 fusion.54
  384.5 3.0 convolution_convert_fusion
  387.5 18.1 %all-to-all-done.5 = f32[4,1,256,640]{2,3,1,0:T(8,128)} async-done(((f32[4,1,256,640]{2,3,1,0:T(8,128)}), f32[4,1,256,640]{2,3,1,0:T(8,128)}, u32[]{:S(2)}, u32[]{:S(2)}) %all-to-all-start.5) | async-done | bytes 2621472 | tf_op jit(solution)/shard_map/all_to_all | solution.py:43
  405.6 2.8 reduce_sum.213
  409.4 2.3 convolution_convert_fusion.6
  412.4 2.3 copy.221
  417.6 2.2 copy.220
  419.8 16.4 %concatenate.52 = bf16[960,4481]{1,0:T(8,128)(2,1)} concatenate(bf16[960,1]{1,0:T(8,128)(2,1)} %convert_element_type.296, bf16[960,960]{1,0:T(8,128)(2,1)S(1)} %convolution_convert_fusion.1, bf16[960,320]{1,0:T(8,128)(2,1)} %copy.220, bf16[960,320]{1,0:T(8,128)(2,1)} %copy.221, bf16[960,960]{1,0:T(8,128)(2,1)} %convolution_convert_fusion, ...), dimensions={1} | concatenate | bytes 17207040 | tf_op jit(solution)/shard_map/concatenate | solution.py:49
  441.0 88.6 %reduce-scatter.2.cloned.1.call-done = bf16[120,4481]{1,0:T(8,128)(2,1)} async-done(((bf16[960,4481]{1,0:T(8,128)(2,1)}), bf16[120,4481]{1,0:T(8,128)(2,1)}) %reduce-scatter.2.cloned.1.call-update) | async-done | bytes 1075456 | tf_op jit(solution)/shard_map/reduce_scatter | solution.py:50
  531.8 4.2 all-to-all-start.8
  536.0 2.1 fusion.72
  538.1 9.2 %all-to-all-done.8 = bf16[4,120,640]{2,1,0:T(8,128)(2,1)} async-done(((bf16[4,120,640]{2,1,0:T(8,128)(2,1)}), bf16[4,120,640]{2,1,0:T(8,128)(2,1)}, u32[]{:S(2)}, u32[]{:S(2)}) %all-to-all-start.8) | async-done | bytes 614432 | tf_op jit(solution)/shard_map/all_to_all | solution.py:22
  548.2 3.5 all-to-all-start.7
  555.5 7.4 %all-to-all-done.7 = bf16[4,120,640]{2,1,0:T(8,128)(2,1)S(1)} async-done(((bf16[4,120,640]{2,1,0:T(8,128)(2,1)}), bf16[4,120,640]{2,1,0:T(8,128)(2,1)S(1)}, u32[]{:S(2)}, u32[]{:S(2)}) %all-to-all-start.7) | async-done | bytes 614432 | tf_op jit(solution)/shard_map/all_to_all | solution.py:22
  563.8 4.2 all-to-all-start.6
  569.1 20.6 %all-reduce.2 = bf16[960]{0:T(1024)(128)(2,1)S(1)} all-reduce(bf16[960]{0:T(1024)(128)(2,1)S(1)} %get-tuple-element.79), channel_id=2, replica_groups=mesh['fsdp'=8,'ctx'=4,'tp'=4] {'fsdp'}, use_global_device_ids=true, to_apply=%region_23.24.clone | all-reduce | flops 960 | bytes 3840
  590.7 34.6 %all-reduce.3 = (bf16[120]{0:T(256)(128)(2,1)S(1)}, bf16[120]{0:T(256)(128)(2,1)S(1)}) all-reduce(bf16[120]{0:T(256)(128)(2,1)S(1)} %dynamic-slice.3, bf16[120]{0:T(256)(128)(2,1)S(1)} %slice_reduce_fusion), channel_id=1, replica_groups=mesh['fsdp'=8,'ctx'=4,'tp'=4] {'ctx','tp'}, use_global_device_ids=true, to_apply=%region_24.25 | all-reduce | flops 240 | bytes 960 | tf_op jit(solution)/shard_map/psum | solution.py:359
  630.9 64.3 %all-reduce.8.cloned.1.call-done = (bf16[120,320]{1,0:T(8,128)(2,1)}, bf16[120,320]{1,0:T(8,128)(2,1)}, bf16[120,960]{1,0:T(8,128)(2,1)}, bf16[120,960]{1,0:T(8,128)(2,1)}) async-done(((bf16[120,320]{1,0:T(8,128)(2,1)}, bf16[120,320]{1,0:T(8,128)(2,1)}, bf16[120,960]{1,0:T(8,128)(2,1)}, bf16[120,960]{1,0:T(8,128)(2,1)}), (bf16[120,320]{1,0:T(8,128)(2,1)}, bf16[120,320]{1,0:T(8,128)(2,1)}, ...) | async-done | bytes 614416 | tf_op jit(solution)/shard_map/psum | solution.py:362
  (239 shorter events, 106.7 us)
Async XLA Ops:
  7.2 137.2 %all-gather.8.cloned.1.call-start = ((), (), s32[]{:S(2)}) async-start(), calls=%async_computation.10 | async-start | bytes 2211840 | tf_op jit(solution)/shard_map/all_gather | solution.py:144
  7.9 155.0 %all-gather.10.cloned.1.call-start = ((), (), s32[]{:S(2)}) async-start(), calls=%async_computation.11 | async-start | bytes 2211840 | tf_op jit(solution)/shard_map/all_gather | solution.py:147
  8.7 194.3 %all-gather.14.cloned.1.call-start = ((), (), s32[]{:S(2)}) async-start(), calls=%async_computation.13 | async-start | bytes 1382400 | tf_op jit(solution)/shard_map/all_gather | solution.py:149
  94.9 2.0 copy-start.25
  95.9 1.9 copy-start.42
  98.3 7.3 %copy-start.38 = (f32[1,256,960]{1,2,0:T(8,128)S(1)}, f32[1,256,960]{1,2,0:T(8,128)}, u32[]{:S(2)}) copy-start(f32[1,256,960]{1,2,0:T(8,128)} %param.25) | copy-start | bytes 2949124
  99.5 32.7 %all-to-all-start = ((bf16[4,1,256,640]{2,3,1,0:T(8,128)(2,1)}), bf16[4,1,256,640]{2,3,1,0:T(8,128)(2,1)S(1)}, u32[]{:S(2)}, u32[]{:S(2)}) async-start(bf16[4,1,256,640]{2,3,1,0:T(8,128)(2,1)} %broadcast_in_dim.38), calls=%async_computation | async-start | bytes 2621440 | tf_op jit(solution)/shard_map/all_to_all | solution.py:22
  104.2 104.1 %all-gather.12.cloned.1.call-start = ((), (), s32[]{:S(2)}) async-start(), calls=%async_computation.12 | async-start | bytes 1382400 | tf_op jit(solution)/shard_map/all_gather | solution.py:148
  105.6 42.8 %copy-start.30 = (pred[256,1024]{0,1:T(8,128)(4,1)}, pred[256,1024]{0,1:T(8,128)(4,1)S(1)}, u32[]{:S(2)}) copy-start(pred[256,1024]{0,1:T(8,128)(4,1)S(1)} %iota_compare_fusion) | copy-start | bytes 786436
  134.6 33.0 %all-to-all-start.3 = ((bf16[4,1,256,960]{2,3,1,0:T(8,128)(2,1)}), bf16[4,1,256,960]{2,3,1,0:T(8,128)(2,1)}, u32[]{:S(2)}, u32[]{:S(2)}) async-start(bf16[4,1,256,960]{2,3,1,0:T(8,128)(2,1)} %broadcast_in_dim.78), calls=%async_computation.3 | async-start | bytes 3932160 | tf_op jit(solution)/shard_map/all_to_all | solution.py:22
  144.4 4.1 copy-start.35
  148.4 3.8 copy-start.10
  148.4 4.6 copy-start.51
  149.2 5.9 copy-start.6
  149.2 2.2 copy-start.31
  149.2 2.3 copy-start.36
  152.3 6.9 copy-start
  153.0 7.4 %copy-start.3 = (f32[1,3,256,1024]{2,3,1,0:T(8,128)}, f32[1,3,256,1024]{2,3,1,0:T(8,128)S(1)}, u32[]{:S(2)}) copy-start(f32[1,3,256,1024]{2,3,1,0:T(8,128)S(1)} %get-tuple-element.122) | copy-start | bytes 9437188
  153.7 7.9 %copy-start.8 = (f32[1,3,256,1024]{2,3,1,0:T(8,128)}, f32[1,3,256,1024]{2,3,1,0:T(8,128)S(1)}, u32[]{:S(2)}) copy-start(f32[1,3,256,1024]{2,3,1,0:T(8,128)S(1)} %get-tuple-element.124) | copy-start | bytes 9437188
  154.2 1.6 copy-start.32
  170.0 28.2 %all-to-all-start.1 = ((bf16[4,1,256,960]{2,3,1,0:T(8,128)(2,1)}), bf16[4,1,256,960]{2,3,1,0:T(8,128)(2,1)}, u32[]{:S(2)}, u32[]{:S(2)}) async-start(bf16[4,1,256,960]{2,3,1,0:T(8,128)(2,1)} %broadcast_in_dim.77), calls=%async_computation.1 | async-start | bytes 3932160 | tf_op jit(solution)/shard_map/all_to_all | solution.py:22
  174.8 44.8 %all-gather.16.cloned.1.call-start = ((), (), s32[]{:S(2)}) async-start(), calls=%async_computation.14 | async-start | bytes 1382400 | tf_op jit(solution)/shard_map/all_gather | solution.py:150
  219.6 8.9 %copy-start.53 = (bf16[960,640]{1,0:T(8,128)(2,1)S(1)}, bf16[960,640]{1,0:T(8,128)(2,1)}, u32[]{:S(2)}) copy-start(bf16[960,640]{1,0:T(8,128)(2,1)} %all-gather.16.cloned.1.call-done) | copy-start | bytes 3686404
  239.2 24.8 %all-to-all-start.2 = ((bf16[4,1,256,960]{2,3,1,0:T(8,128)(2,1)}), bf16[4,1,256,960]{2,3,1,0:T(8,128)(2,1)}, u32[]{:S(2)}, u32[]{:S(2)}) async-start(bf16[4,1,256,960]{2,3,1,0:T(8,128)(2,1)} %copy.199), calls=%async_computation.2 | async-start | bytes 3932160 | tf_op jit(solution)/shard_map/all_to_all | solution.py:37
  243.7 3.6 copy-start.39
  243.7 3.6 copy-start.48
  264.0 44.9 %all-to-all-start.4 = ((f32[4,1,256,960]{2,3,1,0:T(8,128)}), f32[4,1,256,960]{2,3,1,0:T(8,128)}, u32[]{:S(2)}, u32[]{:S(2)}) async-start(f32[4,1,256,960]{2,3,1,0:T(8,128)} %copy.201), calls=%async_computation.4 | async-start | bytes 7864320 | tf_op jit(solution)/shard_map/all_to_all | solution.py:43
  268.9 4.8 copy-start.40
  269.0 4.8 copy-start.46
  273.8 2.7 copy-start.54
  312.3 2.1 copy-start.27
  312.3 2.1 copy-start.29
  314.4 2.9 copy-start.45
  317.4 2.2 copy-start.7
  317.4 3.6 copy-start.9
  317.4 3.6 copy-start.33
  320.9 2.6 copy-start.4
  323.5 2.6 copy-start.1
  331.4 2.7 copy-start.11
  347.3 3.7 copy-start.5
  347.3 4.7 copy-start.24
  351.0 11.8 %copy-start.20 = (bf16[3,256,1024]{1,2,0:T(8,128)(2,1)}, bf16[3,256,1024]{1,2,0:T(8,128)(2,1)S(1)}, u32[]{:S(2)}) copy-start(bf16[3,256,1024]{1,2,0:T(8,128)(2,1)S(1)} %fusion.34) | copy-start | bytes 4718596
  352.0 2.4 copy-start.2
  352.0 3.4 copy-start.23
  352.7 8.7 %copy-start.15 = (bf16[3,256,1024]{1,2,0:T(8,128)(2,1)}, bf16[3,256,1024]{1,2,0:T(8,128)(2,1)S(1)}, u32[]{:S(2)}) copy-start(bf16[3,256,1024]{1,2,0:T(8,128)(2,1)S(1)} %fusion.33) | copy-start | bytes 4718596
  355.5 2.4 copy-start.22
  356.2 4.0 copy-start.17
  358.8 3.9 copy-start.19
  360.1 2.6 copy-start.52
  364.1 2.2 copy-start.34
  368.0 7.5 %copy-start.18 = (bf16[3,256,1024]{1,2,0:T(8,128)(2,1)S(1)}, bf16[3,256,1024]{1,2,0:T(8,128)(2,1)}, u32[]{:S(2)}) copy-start(bf16[3,256,1024]{1,2,0:T(8,128)(2,1)} %copy-done.17) | copy-start | bytes 4718596
  368.0 37.6 %all-to-all-start.5 = ((f32[4,1,256,640]{2,3,1,0:T(8,128)}), f32[4,1,256,640]{2,3,1,0:T(8,128)}, u32[]{:S(2)}, u32[]{:S(2)}) async-start(f32[4,1,256,640]{2,3,1,0:T(8,128)} %pad_maximum_fusion), calls=%async_computation.5 | async-start | bytes 5242880 | tf_op jit(solution)/shard_map/all_to_all | solution.py:43
  372.8 4.7 copy-start.16
  372.8 156.8 %reduce-scatter.2.cloned.1.call-start = ((), (), s32[]{:S(2)}) async-start(), calls=%async_computation.15 | async-start | bytes 9953280 | tf_op jit(solution)/shard_map/reduce_scatter | solution.py:50
  372.8 6.7 copy-start.21
  379.5 4.3 copy-start.26
  381.5 3.0 copy-start.14
  437.7 1.8 copy-start.43
  437.8 1.8 copy-start.50
  439.6 96.4 %copy-start.37 = (f32[256,640]{0,1:T(8,128)S(1)}, f32[256,640]{0,1:T(8,128)}, u32[]{:S(2)}) copy-start(f32[256,640]{0,1:T(8,128)} %reduce_sum.213) | copy-start | bytes 1966084
  531.8 15.5 %all-to-all-start.8 = ((bf16[4,120,640]{2,1,0:T(8,128)(2,1)}), bf16[4,120,640]{2,1,0:T(8,128)(2,1)}, u32[]{:S(2)}, u32[]{:S(2)}) async-start(bf16[4,120,640]{2,1,0:T(8,128)(2,1)} %broadcast_in_dim.81), calls=%async_computation.9 | async-start | bytes 1228800 | tf_op jit(solution)/shard_map/all_to_all | solution.py:22
  548.2 14.7 %all-to-all-start.7 = ((bf16[4,120,640]{2,1,0:T(8,128)(2,1)}), bf16[4,120,640]{2,1,0:T(8,128)(2,1)S(1)}, u32[]{:S(2)}, u32[]{:S(2)}) async-start(bf16[4,120,640]{2,1,0:T(8,128)(2,1)} %broadcast_in_dim.80), calls=%async_computation.8 | async-start | bytes 1228800 | tf_op jit(solution)/shard_map/all_to_all | solution.py:22
  551.7 143.6 %all-reduce.8.cloned.1.call-start = ((), (), s32[]{:S(2)}) async-start(), calls=%async_computation.16 | async-start | bytes 1351680 | tf_op jit(solution)/shard_map/psum | solution.py:362
  563.8 65.2 %all-to-all-start.6 = ((bf16[4,120,640]{2,1,0:T(8,128)(2,1)}), bf16[4,120,640]{2,1,0:T(8,128)(2,1)}, u32[]{:S(2)}, u32[]{:S(2)}) async-start(bf16[4,120,640]{2,1,0:T(8,128)(2,1)} %broadcast_in_dim.79), calls=%async_computation.7 | async-start | bytes 1228800 | tf_op jit(solution)/shard_map/all_to_all | solution.py:22
  (8 other events, 8.3 us)
Sparse Core Ops, SparseCore 0:
  9.6 43.5 all-gather.7
  54.9 41.9 all-gather.9
  98.5 40.3 all-gather.13
  140.5 39.3 all-gather.11
  181.3 38.2 all-gather.15
  436.3 93.1 reduce-scatter.1
  555.8 139.4 all-reduce.7
where the time goes:
time: 716 us; the launch traced here: 709 us
  waiting for transfers between devices  270 us (38%)
  blocking collectives  136 us (19%)
  local copies, waits for them, and re-layouts  102 us (14%)
  matrix products  102 us (14%)
  starting transfers between devices  41.3 us (6%)
  other arithmetic  41.3 us (6%)
  between operations  17.3 us (2%)
    reduce_scatter x1, waiting for transfers between devices, sent_together(): lax.psum_scatter(both, axis, scatter_dimension=dim, tiled=True)  88.6 us
    psum x1, waiting for transfers between devices, shards(): lax.psum(share_key.astype(jnp.bfloat16), ('ctx', 'tp')).astype(jnp.float32)  64.3 us
    all_to_all x6, waiting for transfers between devices, from_everyone(): return lax.all_to_all(copies, axis, split_axis=0, concat_axis=0, tiled=True)  60.2 us
    all_to_all x2, waiting for transfers between devices, sum_at_owner(): lax.all_to_all(tiles, axis, split_axis=0, concat_axis=0, tiled=True)  44.8 us
    unnamed x2, blocking collectives  38.9 us
    psum x1, blocking collectives, shards(): lax.psum(share_gain_one.astype(jnp.bfloat16), ('ctx', 'tp'))  34.6 us
    all_gather x1, blocking collectives, shards(): lax.all_gather(w_key, 'fsdp', axis=0, tiled=True)  31.9 us
    all_gather x1, blocking collectives, shards(): lax.all_gather(w_value, 'fsdp', axis=0, tiled=True)  31 us
  transfers between devices with their start and end apart: 16, of which 10 were waited for; matrix products, arithmetic and copies ran while one was open for 17% of the time, Pallas kernels for 0%

commit v1 on v0

--- a/solution.py
+++ b/solution.py
@@ -355,8 +355,9 @@
         over_copies(share_up.astype(jnp.bfloat16), "ctx").astype(jnp.float32),
         over_copies(share_down.astype(jnp.bfloat16), "ctx").astype(jnp.float32),
     )
+    sides_get = lambda patch: jnp.sum(jax.lax.all_gather(patch, axis_name=("ctx", "tp")), axis=0)
     share_gain_one, share_gain_two, share_query, share_key, share_value, share_out = (
-        lax.psum(share_gain_one.astype(jnp.bfloat16), ("ctx", "tp")).astype(jnp.float32),
+        sides_get(share_gain_one.astype(jnp.bfloat16)).astype(jnp.float32),
         lax.psum(share_gain_two.astype(jnp.bfloat16), ("ctx", "tp")).astype(jnp.float32),
         lax.psum(share_query.astype(jnp.bfloat16), ("ctx", "tp")).astype(jnp.float32),
         lax.psum(share_key.astype(jnp.bfloat16), ("ctx", "tp")).astype(jnp.float32),

time: 716 us -> 716 us (level)
    unnamed x2 -> x3, blocking collectives: 38.9 us -> 74 us
    psum x1 -> x0, blocking collectives: 34.6 us -> none  [shards(): lax.psum(share_gain_one.astype(jnp.bfloat16), ('ctx', 'tp'))]
    unnamed x124 -> x129, local copies, waits for them, and re-layouts: 24.1 us -> 24.8 us
where the time goes in v1:
time: 716 us; the launch traced here: 709 us
  waiting for transfers between devices  268 us (37%)
  blocking collectives  137 us (19%)
  local copies, waits for them, and re-layouts  102 us (14%)
  matrix products  102 us (14%)
  starting transfers between devices  41.3 us (6%)
  other arithmetic  41.3 us (6%)
  between operations  17.9 us (2%)
    reduce_scatter x1, waiting for transfers between devices, sent_together(): lax.psum_scatter(both, axis, scatter_dimension=dim, tiled=True)  87.6 us
    unnamed x3, blocking collectives  74 us
    psum x1, waiting for transfers between devices, shards(): lax.psum(share_key.astype(jnp.bfloat16), ('ctx', 'tp')).astype(jnp.float32)  63.5 us
    all_to_all x6, waiting for transfers between devices, from_everyone(): return lax.all_to_all(copies, axis, split_axis=0, concat_axis=0, tiled=True)  60.2 us
    all_to_all x2, waiting for transfers between devices, sum_at_owner(): lax.all_to_all(tiles, axis, split_axis=0, concat_axis=0, tiled=True)  44.9 us
    all_gather x1, blocking collectives, shards(): lax.all_gather(w_key, 'fsdp', axis=0, tiled=True)  31.9 us
    all_gather x1, blocking collectives, shards(): lax.all_gather(w_value, 'fsdp', axis=0, tiled=True)  31 us
    all_to_all x6, starting transfers between devices, from_everyone(): return lax.all_to_all(copies, axis, split_axis=0, concat_axis=0, tiled=True)  26.5 us
  transfers between devices with their start and end apart: 16, of which 10 were waited for; matrix products, arithmetic and copies ran while one was open for 17% of the time, Pallas kernels for 0%

profile of v1, /device:TPU:0, one launch (start us, length us, event | category | flops | bytes accessed | tf_op | source)
XLA Modules:
  0.0 709.2 jit_solution(7344623231868554522)
XLA Ops:
  9.4 31.9 %all-gather.1 = bf16[8,120,320]{1,2,0:T(8,128)(2,1)S(1)} all-gather(bf16[1,120,320]{1,2,0:T(8,128)(2,1)} %bitcast.613), channel_id=1, replica_groups=mesh['fsdp'=8,'ctx'=4,'tp'=4] {'fsdp'}, dimensions={0}, use_global_device_ids=true | all-gather | bytes 691200 | tf_op jit(solution)/shard_map/all_gather | solution.py:145
  41.3 31.0 %all-gather.2 = bf16[8,120,320]{1,2,0:T(8,128)(2,1)S(1)} all-gather(bf16[1,120,320]{1,2,0:T(8,128)(2,1)} %bitcast.614), channel_id=1, replica_groups=mesh['fsdp'=8,'ctx'=4,'tp'=4] {'fsdp'}, dimensions={0}, use_global_device_ids=true | all-gather | bytes 691200 | tf_op jit(solution)/shard_map/all_gather | solution.py:146
  76.7 18.3 %all-reduce.6 = (bf16[960]{0:T(1024)(128)(2,1)S(1)}, bf16[960]{0:T(1024)(128)(2,1)S(1)}) all-reduce(bf16[960]{0:T(1024)(128)(2,1)S(1)} %dynamic-update-slice, bf16[960]{0:T(1024)(128)(2,1)S(1)} %dynamic-update-slice.1), channel_id=1, replica_groups=mesh['fsdp'=8,'ctx'=4,'tp'=4] {'fsdp'}, use_global_device_ids=true, to_apply=%add | all-reduce | flops 1920 | bytes 7680
  99.5 4.7 all-to-all-start
  106.5 25.6 %all-to-all-done = bf16[4,1,256,640]{2,3,1,0:T(8,128)(2,1)S(1)} async-done(((bf16[4,1,256,640]{2,3,1,0:T(8,128)(2,1)}), bf16[4,1,256,640]{2,3,1,0:T(8,128)(2,1)S(1)}, u32[]{:S(2)}, u32[]{:S(2)}) %all-to-all-start) | async-done | bytes 1310752 | tf_op jit(solution)/shard_map/all_to_all | solution.py:22
  132.1 2.4 broadcast_in_dim.78
  134.6 5.3 all-to-all-start.3
  141.8 2.3 copy.190
  144.4 3.1 copy.192
  149.2 2.2 fusion.128
  162.9 2.7 multiply_reduce_fusion.2
  167.6 2.4 broadcast_in_dim.77
  170.0 4.8 all-to-all-start.1
  175.3 3.1 copy.200
  180.2 18.0 %all-to-all-done.1 = bf16[4,1,256,960]{2,3,1,0:T(8,128)(2,1)} async-done(((bf16[4,1,256,960]{2,3,1,0:T(8,128)(2,1)}), bf16[4,1,256,960]{2,3,1,0:T(8,128)(2,1)}, u32[]{:S(2)}, u32[]{:S(2)}) %all-to-all-start.1) | async-done | bytes 1966112 | tf_op jit(solution)/shard_map/all_to_all | solution.py:22
  198.2 3.1 copy.198
  203.0 5.3 fusion.133
  208.3 5.2 fusion.132
  213.5 6.0 all-gather.17.cloned.1.call-done
  219.5 7.8 %multiply_convert_fusion = (bf16[1024,640]{1,0:T(8,128)(2,1)}, bf16[1024,640]{1,0:T(8,128)(2,1)}, bf16[1024,640]{1,0:T(8,128)(2,1)S(1)}) fusion(f32[1024,640]{1,0:T(8,128)} %fusion.132, f32[1024,640]{1,0:T(8,128)} %fusion.133, bf16[1024,960]{0,1:T(8,128)(2,1)} %bitcast.599, bf16[960,640]{1,0:T(8,128)(2,1)} %all-gather.17.cloned.1.call-done), kind=kOutput, calls=%fused_computation.47 | convolution fusion | flops 1268776960 | bytes 12369920 | tf_op jit(solution)/shard_map/dot_general | solution.py:225
  228.4 3.0 convolution_convert_fusion.2
  231.4 4.7 convert_element_type.262
  236.1 3.1 copy.199
  239.2 4.5 all-to-all-start.2
  243.7 3.6 fusion.134
  247.3 3.6 convolution_add_fusion
  250.9 5.5 reshape_reshape.11
  256.3 4.7 copy.201
  261.0 2.9 all-to-all-done.2
  263.9 5.0 all-to-all-start.4
  268.9 4.8 convolution_convert_fusion.3
  273.7 2.7 convolution_convert_fusion.4
  276.5 2.8 convolution_convert_fusion.5
  279.2 2.9 convert_reduce_fusion
  282.1 26.7 %all-to-all-done.4 = f32[4,1,256,960]{2,3,1,0:T(8,128)} async-done(((f32[4,1,256,960]{2,3,1,0:T(8,128)}), f32[4,1,256,960]{2,3,1,0:T(8,128)}, u32[]{:S(2)}, u32[]{:S(2)}) %all-to-all-start.4) | async-done | bytes 3932192 | tf_op jit(solution)/shard_map/all_to_all | solution.py:43
  308.9 3.4 reduce_sum.218
  312.3 2.0 multiply_reduce_fusion
  314.4 2.9 bitcast_add_fusion
  320.9 2.3 fusion
  323.5 2.3 fusion.4
  326.2 2.3 fusion.8
  328.5 2.3 fusion.12
  341.8 2.8 concatenate.49
  344.6 2.6 copy.218
  347.3 3.7 fusion.34
  368.0 4.7 all-to-all-start.5
  372.8 2.7 fusion.54
  384.4 3.0 convolution_convert_fusion
  387.5 18.1 %all-to-all-done.5 = f32[4,1,256,640]{2,3,1,0:T(8,128)} async-done(((f32[4,1,256,640]{2,3,1,0:T(8,128)}), f32[4,1,256,640]{2,3,1,0:T(8,128)}, u32[]{:S(2)}, u32[]{:S(2)}) %all-to-all-start.5) | async-done | bytes 2621472 | tf_op jit(solution)/shard_map/all_to_all | solution.py:43
  405.6 2.8 reduce_sum.225
  409.4 2.3 convolution_convert_fusion.6
  412.4 2.3 copy.221
  417.6 2.2 copy.220
  419.8 16.3 %concatenate.52 = bf16[960,4481]{1,0:T(8,128)(2,1)} concatenate(bf16[960,1]{1,0:T(8,128)(2,1)} %convert_element_type.298, bf16[960,960]{1,0:T(8,128)(2,1)S(1)} %convolution_convert_fusion.1, bf16[960,320]{1,0:T(8,128)(2,1)} %copy.220, bf16[960,320]{1,0:T(8,128)(2,1)} %copy.221, bf16[960,960]{1,0:T(8,128)(2,1)} %convolution_convert_fusion, ...), dimensions={1} | concatenate | bytes 17207040 | tf_op jit(solution)/shard_map/concatenate | solution.py:49
  442.0 87.6 %reduce-scatter.2.cloned.1.call-done = bf16[120,4481]{1,0:T(8,128)(2,1)} async-done(((bf16[960,4481]{1,0:T(8,128)(2,1)}), bf16[120,4481]{1,0:T(8,128)(2,1)}) %reduce-scatter.2.cloned.1.call-update) | async-done | bytes 1075456 | tf_op jit(solution)/shard_map/reduce_scatter | solution.py:50
  531.8 4.2 all-to-all-start.8
  535.9 2.1 fusion.72
  538.1 9.2 %all-to-all-done.8 = bf16[4,120,640]{2,1,0:T(8,128)(2,1)} async-done(((bf16[4,120,640]{2,1,0:T(8,128)(2,1)}), bf16[4,120,640]{2,1,0:T(8,128)(2,1)}, u32[]{:S(2)}, u32[]{:S(2)}) %all-to-all-start.8) | async-done | bytes 614432 | tf_op jit(solution)/shard_map/all_to_all | solution.py:22
  548.1 3.5 all-to-all-start.7
  555.5 7.4 %all-to-all-done.7 = bf16[4,120,640]{2,1,0:T(8,128)(2,1)S(1)} async-done(((bf16[4,120,640]{2,1,0:T(8,128)(2,1)}), bf16[4,120,640]{2,1,0:T(8,128)(2,1)S(1)}, u32[]{:S(2)}, u32[]{:S(2)}) %all-to-all-start.7) | async-done | bytes 614432 | tf_op jit(solution)/shard_map/all_to_all | solution.py:22
  563.8 4.1 all-to-all-start.6
  569.1 20.6 %all-reduce.3 = bf16[960]{0:T(1024)(128)(2,1)S(1)} all-reduce(bf16[960]{0:T(1024)(128)(2,1)S(1)} %get-tuple-element.79), channel_id=3, replica_groups=mesh['fsdp'=8,'ctx'=4,'tp'=4] {'fsdp'}, use_global_device_ids=true, to_apply=%region_23.24.clone | all-reduce | flops 960 | bytes 3840
  590.8 35.1 %all-reduce.4 = (bf16[1920]{0:T(1024)(128)(2,1)S(1)}, bf16[120]{0:T(256)(128)(2,1)S(1)}) all-reduce(bf16[1920]{0:T(1024)(128)(2,1)S(1)} %dynamic-update-slice.2, bf16[120]{0:T(256)(128)(2,1)S(1)} %slice_reduce_fusion), channel_id=2, replica_groups=mesh['fsdp'=8,'ctx'=4,'tp'=4] {'ctx','tp'}, use_global_device_ids=true, to_apply=%add.2 | all-reduce | flops 2040 | bytes 8160
  631.7 63.5 %all-reduce.9.cloned.1.call-done = (bf16[120,320]{1,0:T(8,128)(2,1)}, bf16[120,320]{1,0:T(8,128)(2,1)}, bf16[120,960]{1,0:T(8,128)(2,1)}, bf16[120,960]{1,0:T(8,128)(2,1)}) async-done(((bf16[120,320]{1,0:T(8,128)(2,1)}, bf16[120,320]{1,0:T(8,128)(2,1)}, bf16[120,960]{1,0:T(8,128)(2,1)}, bf16[120,960]{1,0:T(8,128)(2,1)}), (bf16[120,320]{1,0:T(8,128)(2,1)}, bf16[120,320]{1,0:T(8,128)(2,1)}, ...) | async-done | bytes 614416 | tf_op jit(solution)/shard_map/psum | solution.py:363
  (246 shorter events, 107.5 us)
Async XLA Ops:
  7.2 137.2 %all-gather.9.cloned.1.call-start = ((), (), s32[]{:S(2)}) async-start(), calls=%async_computation.10 | async-start | bytes 2211840 | tf_op jit(solution)/shard_map/all_gather | solution.py:144
  7.9 155.0 %all-gather.11.cloned.1.call-start = ((), (), s32[]{:S(2)}) async-start(), calls=%async_computation.11 | async-start | bytes 2211840 | tf_op jit(solution)/shard_map/all_gather | solution.py:147
  8.7 194.3 %all-gather.15.cloned.1.call-start = ((), (), s32[]{:S(2)}) async-start(), calls=%async_computation.13 | async-start | bytes 1382400 | tf_op jit(solution)/shard_map/all_gather | solution.py:149
  94.9 2.0 copy-start.25
  95.9 1.9 copy-start.42
  98.3 7.3 %copy-start.38 = (f32[1,256,960]{1,2,0:T(8,128)S(1)}, f32[1,256,960]{1,2,0:T(8,128)}, u32[]{:S(2)}) copy-start(f32[1,256,960]{1,2,0:T(8,128)} %param.25) | copy-start | bytes 2949124
  99.5 32.7 %all-to-all-start = ((bf16[4,1,256,640]{2,3,1,0:T(8,128)(2,1)}), bf16[4,1,256,640]{2,3,1,0:T(8,128)(2,1)S(1)}, u32[]{:S(2)}, u32[]{:S(2)}) async-start(bf16[4,1,256,640]{2,3,1,0:T(8,128)(2,1)} %broadcast_in_dim.38), calls=%async_computation | async-start | bytes 2621440 | tf_op jit(solution)/shard_map/all_to_all | solution.py:22
  104.2 104.1 %all-gather.13.cloned.1.call-start = ((), (), s32[]{:S(2)}) async-start(), calls=%async_computation.12 | async-start | bytes 1382400 | tf_op jit(solution)/shard_map/all_gather | solution.py:148
  105.6 42.8 %copy-start.30 = (pred[256,1024]{0,1:T(8,128)(4,1)}, pred[256,1024]{0,1:T(8,128)(4,1)S(1)}, u32[]{:S(2)}) copy-start(pred[256,1024]{0,1:T(8,128)(4,1)S(1)} %iota_compare_fusion) | copy-start | bytes 786436
  134.6 33.0 %all-to-all-start.3 = ((bf16[4,1,256,960]{2,3,1,0:T(8,128)(2,1)}), bf16[4,1,256,960]{2,3,1,0:T(8,128)(2,1)}, u32[]{:S(2)}, u32[]{:S(2)}) async-start(bf16[4,1,256,960]{2,3,1,0:T(8,128)(2,1)} %broadcast_in_dim.78), calls=%async_computation.3 | async-start | bytes 3932160 | tf_op jit(solution)/shard_map/all_to_all | solution.py:22
  144.4 4.1 copy-start.35
  148.4 3.8 copy-start.10
  148.4 4.6 copy-start.51
  149.2 5.9 copy-start.6
  149.2 2.2 copy-start.31
  149.2 2.3 copy-start.36
  152.3 6.9 copy-start
  153.0 7.4 %copy-start.3 = (f32[1,3,256,1024]{2,3,1,0:T(8,128)}, f32[1,3,256,1024]{2,3,1,0:T(8,128)S(1)}, u32[]{:S(2)}) copy-start(f32[1,3,256,1024]{2,3,1,0:T(8,128)S(1)} %get-tuple-element.122) | copy-start | bytes 9437188
  153.7 7.9 %copy-start.8 = (f32[1,3,256,1024]{2,3,1,0:T(8,128)}, f32[1,3,256,1024]{2,3,1,0:T(8,128)S(1)}, u32[]{:S(2)}) copy-start(f32[1,3,256,1024]{2,3,1,0:T(8,128)S(1)} %get-tuple-element.124) | copy-start | bytes 9437188
  170.0 28.2 %all-to-all-start.1 = ((bf16[4,1,256,960]{2,3,1,0:T(8,128)(2,1)}), bf16[4,1,256,960]{2,3,1,0:T(8,128)(2,1)}, u32[]{:S(2)}, u32[]{:S(2)}) async-start(bf16[4,1,256,960]{2,3,1,0:T(8,128)(2,1)} %broadcast_in_dim.77), calls=%async_computation.1 | async-start | bytes 3932160 | tf_op jit(solution)/shard_map/all_to_all | solution.py:22
  174.8 44.8 %all-gather.17.cloned.1.call-start = ((), (), s32[]{:S(2)}) async-start(), calls=%async_computation.14 | async-start | bytes 1382400 | tf_op jit(solution)/shard_map/all_gather | solution.py:150
  219.5 8.9 %copy-start.53 = (bf16[960,640]{1,0:T(8,128)(2,1)S(1)}, bf16[960,640]{1,0:T(8,128)(2,1)}, u32[]{:S(2)}) copy-start(bf16[960,640]{1,0:T(8,128)(2,1)} %all-gather.17.cloned.1.call-done) | copy-start | bytes 3686404
  239.2 24.8 %all-to-all-start.2 = ((bf16[4,1,256,960]{2,3,1,0:T(8,128)(2,1)}), bf16[4,1,256,960]{2,3,1,0:T(8,128)(2,1)}, u32[]{:S(2)}, u32[]{:S(2)}) async-start(bf16[4,1,256,960]{2,3,1,0:T(8,128)(2,1)} %copy.199), calls=%async_computation.2 | async-start | bytes 3932160 | tf_op jit(solution)/shard_map/all_to_all | solution.py:37
  243.7 3.6 copy-start.39
  243.7 3.6 copy-start.48
  263.9 44.9 %all-to-all-start.4 = ((f32[4,1,256,960]{2,3,1,0:T(8,128)}), f32[4,1,256,960]{2,3,1,0:T(8,128)}, u32[]{:S(2)}, u32[]{:S(2)}) async-start(f32[4,1,256,960]{2,3,1,0:T(8,128)} %copy.201), calls=%async_computation.4 | async-start | bytes 7864320 | tf_op jit(solution)/shard_map/all_to_all | solution.py:43
  268.9 4.8 copy-start.40
  268.9 4.8 copy-start.46
  273.7 2.7 copy-start.55
  312.3 2.1 copy-start.27
  312.3 2.1 copy-start.29
  314.4 2.9 copy-start.45
  317.3 2.2 copy-start.7
  317.3 3.6 copy-start.9
  317.3 3.6 copy-start.33
  320.9 2.6 copy-start.4
  323.5 2.6 copy-start.1
  331.4 2.7 copy-start.11
  347.3 3.7 copy-start.5
  347.3 4.7 copy-start.24
  350.9 11.8 %copy-start.20 = (bf16[3,256,1024]{1,2,0:T(8,128)(2,1)}, bf16[3,256,1024]{1,2,0:T(8,128)(2,1)S(1)}, u32[]{:S(2)}) copy-start(bf16[3,256,1024]{1,2,0:T(8,128)(2,1)S(1)} %fusion.34) | copy-start | bytes 4718596
  352.0 2.4 copy-start.2
  352.0 3.4 copy-start.23
  352.7 8.7 %copy-start.15 = (bf16[3,256,1024]{1,2,0:T(8,128)(2,1)}, bf16[3,256,1024]{1,2,0:T(8,128)(2,1)S(1)}, u32[]{:S(2)}) copy-start(bf16[3,256,1024]{1,2,0:T(8,128)(2,1)S(1)} %fusion.33) | copy-start | bytes 4718596
  355.4 2.4 copy-start.22
  356.1 4.0 copy-start.17
  358.8 3.9 copy-start.19
  360.1 2.6 copy-start.52
  364.1 2.2 copy-start.34
  368.0 7.5 %copy-start.18 = (bf16[3,256,1024]{1,2,0:T(8,128)(2,1)S(1)}, bf16[3,256,1024]{1,2,0:T(8,128)(2,1)}, u32[]{:S(2)}) copy-start(bf16[3,256,1024]{1,2,0:T(8,128)(2,1)} %copy-done.17) | copy-start | bytes 4718596
  368.0 37.6 %all-to-all-start.5 = ((f32[4,1,256,640]{2,3,1,0:T(8,128)}), f32[4,1,256,640]{2,3,1,0:T(8,128)}, u32[]{:S(2)}, u32[]{:S(2)}) async-start(f32[4,1,256,640]{2,3,1,0:T(8,128)} %pad_maximum_fusion), calls=%async_computation.5 | async-start | bytes 5242880 | tf_op jit(solution)/shard_map/all_to_all | solution.py:43
  372.7 4.7 copy-start.16
  372.7 156.8 %reduce-scatter.2.cloned.1.call-start = ((), (), s32[]{:S(2)}) async-start(), calls=%async_computation.15 | async-start | bytes 9953280 | tf_op jit(solution)/shard_map/reduce_scatter | solution.py:50
  372.8 6.7 copy-start.21
  379.4 4.3 copy-start.26
  381.5 3.0 copy-start.14
  436.2 2.5 copy-start.44
  438.7 1.8 copy-start.43
  438.7 1.8 copy-start.50
  440.5 95.4 %copy-start.37 = (f32[256,640]{0,1:T(8,128)S(1)}, f32[256,640]{0,1:T(8,128)}, u32[]{:S(2)}) copy-start(f32[256,640]{0,1:T(8,128)} %reduce_sum.225) | copy-start | bytes 1966084
  531.8 15.5 %all-to-all-start.8 = ((bf16[4,120,640]{2,1,0:T(8,128)(2,1)}), bf16[4,120,640]{2,1,0:T(8,128)(2,1)}, u32[]{:S(2)}, u32[]{:S(2)}) async-start(bf16[4,120,640]{2,1,0:T(8,128)(2,1)} %broadcast_in_dim.81), calls=%async_computation.9 | async-start | bytes 1228800 | tf_op jit(solution)/shard_map/all_to_all | solution.py:22
  548.1 14.7 %all-to-all-start.7 = ((bf16[4,120,640]{2,1,0:T(8,128)(2,1)}), bf16[4,120,640]{2,1,0:T(8,128)(2,1)S(1)}, u32[]{:S(2)}, u32[]{:S(2)}) async-start(bf16[4,120,640]{2,1,0:T(8,128)(2,1)} %broadcast_in_dim.80), calls=%async_computation.8 | async-start | bytes 1228800 | tf_op jit(solution)/shard_map/all_to_all | solution.py:22
  551.6 143.6 %all-reduce.9.cloned.1.call-start = ((), (), s32[]{:S(2)}) async-start(), calls=%async_computation.16 | async-start | bytes 1351680 | tf_op jit(solution)/shard_map/psum | solution.py:363
  563.8 66.1 %all-to-all-start.6 = ((bf16[4,120,640]{2,1,0:T(8,128)(2,1)}), bf16[4,120,640]{2,1,0:T(8,128)(2,1)}, u32[]{:S(2)}, u32[]{:S(2)}) async-start(bf16[4,120,640]{2,1,0:T(8,128)(2,1)} %broadcast_in_dim.79), calls=%async_computation.7 | async-start | bytes 1228800 | tf_op jit(solution)/shard_map/all_to_all | solution.py:22
  (9 other events, 9.0 us)
Sparse Core Ops, SparseCore 0:
  9.6 43.5 all-gather.8
  54.9 41.9 all-gather.10
  98.5 40.3 all-gather.14
  140.5 39.3 all-gather.12
  181.3 38.1 all-gather.16
  436.3 93.1 reduce-scatter.1
  555.7 139.4 all-reduce.8
